TPU v7x, 256 devices: a whole 4x4x8 slice. The times are simulated.
256 devices in a mesh: section: 4 (over x_hi, core), tile: 64 (over z, x_lo, y).
Axes of the slice: x: 4 (x_hi: 2, x_lo: 2; x = x_hi * 2 + x_lo), y: 4, z: 8, core: 2. Of those that a mesh axis runs over, the one named last changes fastest.
Arguments:
- saved: float32 [4, 5, 8, 512, 128], P('section', None, None, 'tile'), may hold values from -2.5 to 2.5
- sched: int32 [4], replicated, may hold values from 0 to 3, each once
Outputs:
- gradient: float32 [5, 8, 512, 128], P(None, None, 'tile')
Inputs may be any that keep to these rules, and one draw needn't show every extreme that they name: sched is a permutation of 0 .. 3.
All inputs are finite; a program needn't handle non-finite values.
Results may differ from a plain program's by a relative error of at most 0.0001.
Values sent between devices are 32-bit elements; how exact they have to be, the bound alone decides.
A program may use at most 64 MiB of HBM per device.

v0:
```python
import jax
import jax.numpy as jnp
from jax import lax
from jax.experimental import pallas as pl
from jax.experimental.pallas import tpu as pltpu
from jax.sharding import PartitionSpec as P

MESH = pl.DeviceIdType.MESH

DT = 0.1
HYPER = 0.1
HALO = 12
EDGE = 6
TILE = 8
ROWS = TILE + 2 * HALO
LROWS = TILE + 2 * EDGE
U, V, W, B, PR = range(5)

D8 = 8.0 / 12.0
D1 = 1.0 / 12.0
C1 = DT * HYPER
C4 = 4.0 * C1
C0 = 18.0 * C1


def lanes(v, k):
    return pltpu.roll(v, (-k) % 128, 1)


def planes(v, k):
    return pltpu.roll(v, (-k) % 8, 0)


def slope_parts(p1, m1, p2, m2):
    return D8 * (p1 - m1) - D1 * (p2 - m2)


def forward_row(src, i, slopes, want_rate):
    mid = [src[f, i] for f in range(5)]
    vel = mid[:3]
    rate = [None] * 5
    dxs, dys, dzs = [], [], []
    for f in range(5):
        q = mid[f]
        xp1, xm1, xp2, xm2 = src[f, i + 1], src[f, i - 1], src[f, i + 2], src[f, i - 2]
        yp1, ym1, yp2, ym2 = lanes(q, 1), lanes(q, -1), lanes(q, 2), lanes(q, -2)
        zp1, zm1, zp2, zm2 = planes(q, 1), planes(q, -1), planes(q, 2), planes(q, -2)
        dx = slope_parts(xp1, xm1, xp2, xm2)
        dy = slope_parts(yp1, ym1, yp2, ym2)
        dz = slope_parts(zp1, zm1, zp2, zm2)
        dxs.append(dx)
        dys.append(dy)
        dzs.append(dz)
        if slopes is not None and f < 4:
            slopes[f, i] = dx
            slopes[4 + f, i] = dy
            slopes[8 + f, i] = dz
        if want_rate:
            near = ((xp1 + xm1) + (yp1 + ym1)) + (zp1 + zm1)
            far = ((xp2 + xm2) + (yp2 + ym2)) + (zp2 + zm2)
            rate[f] = C4 * near - C1 * far - C0 * q
    if not want_rate:
        return None, None
    vd = [DT * c for c in vel]
    for f in range(4):
        rate[f] = rate[f] - (vd[0] * dxs[f] + vd[1] * dys[f] + vd[2] * dzs[f])
    rate[U] = rate[U] - DT * dxs[PR]
    rate[V] = rate[V] - DT * dys[PR]
    rate[W] = rate[W] - DT * (dzs[PR] - mid[B])
    rate[B] = rate[B] - vd[2]
    rate[PR] = rate[PR] - DT * ((dxs[U] + dys[V]) + dzs[W])
    return mid, rate


def transposed_row(adj, at, base, slopes, i):
    a = [adj[f, at] for f in range(5)]
    u_rows = {k: base[U, i + k] for k in (-2, -1, 1, 2)}
    u8p, u8m = (DT * D8) * u_rows[1], (DT * D8) * u_rows[-1]
    u1p, u1m = (DT * D1) * u_rows[2], (DT * D1) * u_rows[-2]
    v, w = base[V, i], base[W, i]
    v8, v1 = (DT * D8) * v, (DT * D1) * v
    w8, w1 = (DT * D8) * w, (DT * D1) * w
    ap = {k: adj[PR, at + k] for k in (-2, -1, 1, 2)}
    out = []
    for f in range(5):
        q = a[f]
        row = ap if f == PR else {k: adj[f, at + k] for k in (-2, -1, 1, 2)}
        total = C4 * (row[1] + row[-1]) - C1 * (row[2] + row[-2]) - C0 * q
        if f < 4:
            total = total + ((u8p * row[1] - u8m * row[-1]) - (u1p * row[2] - u1m * row[-2]))
            if f == U:
                total = total + ((DT * D8) * (ap[1] - ap[-1]) - (DT * D1) * (ap[2] - ap[-2]))
        else:
            au = {k: adj[U, at + k] for k in (-2, -1, 1, 2)}
            total = total + ((DT * D8) * (au[1] - au[-1]) - (DT * D1) * (au[2] - au[-2]))
        near, far = C4 * q, C1 * q
        if f < 4:
            p8, p1 = v8 * q, v1 * q
            if f == V:
                p8, p1 = p8 + (DT * D8) * a[PR], p1 + (DT * D1) * a[PR]
        else:
            p8, p1 = (DT * D8) * a[V], (DT * D1) * a[V]
        total = total + (lanes(near + p8, 1) + lanes(near - p8, -1))
        total = total - (lanes(far + p1, 2) + lanes(far - p1, -2))
        if f < 4:
            p8, p1 = w8 * q, w1 * q
            if f == W:
                p8, p1 = p8 + (DT * D8) * a[PR], p1 + (DT * D1) * a[PR]
        else:
            p8, p1 = (DT * D8) * a[W], (DT * D1) * a[W]
        total = total + (planes(near + p8, 1) + planes(near - p8, -1))
        total = total - (planes(far + p1, 2) + planes(far - p1, -2))
        out.append(total)
    ad = [DT * c for c in a[:4]]
    for d in range(3):
        s = ad[0] * slopes[4 * d, i] + ad[1] * slopes[4 * d + 1, i]
        s = s + (ad[2] * slopes[4 * d + 2, i] + ad[3] * slopes[4 * d + 3, i])
        out[d] = out[d] - s
    out[W] = out[W] - ad[3]
    out[B] = out[B] + ad[2]
    return a, out


def rows_loop(lo, hi, body):
    def step(j, carry):
        i = lo + 2 * j
        body(i)
        body(i + 1)
        return carry

    lax.fori_loop(0, (hi - lo) // 2, step, 0)


def first_stages(state, first, second, s0, s1, reach):
    def one(i):
        mid, rate = forward_row(state, i, s0, True)
        for f in range(5):
            first[f, i] = mid[f] + rate[f]

    rows_loop(HALO - reach - 2, HALO + TILE + reach + 2, one)

    def two(i):
        mid, rate = forward_row(first, i, s1, True)
        for f in range(5):
            second[f, i] = 0.75 * state[f, i] + 0.25 * (mid[f] + rate[f])

    rows_loop(HALO - reach, HALO + TILE + reach, two)


def last_slopes(second, s2):
    def three(i):
        forward_row(second, i, s2, False)

    rows_loop(HALO - 4, HALO + TILE + 4, three)


def misfit(state, second, s2, target, lam):
    def three(i):
        mid, rate = forward_row(second, i, s2, True)
        at = i - (HALO - EDGE)
        for f in range(5):
            end = state[f, i] / 3.0 + (2.0 / 3.0) * (mid[f] + rate[f])
            lam[f, at] = end - target[f, at]

    rows_loop(HALO - EDGE, HALO + TILE + EDGE, three)


def transposed_step(state, first, second, s0, s1, s2, lam, g2, g1, emit):
    shift = HALO - EDGE

    def three(i):
        a, out = transposed_row(lam, i - shift, second, s2, i)
        for f in range(5):
            g2[f, i - shift] = (2.0 / 3.0) * (a[f] + out[f])

    rows_loop(HALO - 4, HALO + TILE + 4, three)

    def two(i):
        a, out = transposed_row(g2, i - shift, first, s1, i)
        for f in range(5):
            g1[f, i - shift] = 0.25 * (a[f] + out[f])

    rows_loop(HALO - 2, HALO + TILE + 2, two)

    def one(i):
        at = i - shift
        a, out = transposed_row(g1, at, state, s0, i)
        for f in range(5):
            emit(f, i - HALO, lam[f, at] / 3.0 + 0.75 * g2[f, at] + (a[f] + out[f]))

    rows_loop(HALO, HALO + TILE, one)


def kernel(tiles, sched, saved, out, slots, ext, ext0, goal, first, second, slopes, first0, second0, slopes0, lam, lam1, done2, done1, g2, g1,
           own_sem, gs, gr, es, er, e0s, e0r, ts, tr, as_, ar, bs, br, fs, fr):
    sec, tile = lax.axis_index("section"), lax.axis_index("tile")
    core = lax.rem(sec, 2)
    mate = sec + 1 - 2 * core
    half = lax.div(sec, 2)
    across = sec + 2 - 4 * half
    near = {k: lax.rem(tile + tiles + k, tiles) for k in (-2, -1, 1, 2)}

    own = pltpu.make_async_copy(saved, slots.at[sec], own_sem)
    own.start()

    barrier = pltpu.get_barrier_semaphore()
    partners = [(mate, tile), (across, tile)] + [(sec, near[k]) for k in (-2, -1, 1, 2)] + [(mate, near[k]) for k in (-1, 1)]
    for who in partners:
        pl.semaphore_signal(barrier, inc=1, device_id=who, device_id_type=MESH)
    pl.semaphore_wait(barrier, len(partners))

    def send(src, dst, s, r, who):
        return pltpu.make_async_remote_copy(src_ref=src, dst_ref=dst, send_sem=s, recv_sem=r, device_id=who, device_id_type=MESH)

    to_across = send(saved, slots.at[sec], gs.at[0], gr.at[0], (across, tile))
    to_mate = send(saved, slots.at[sec], gs.at[1], gr.at[1], (mate, tile))
    to_across.start()
    to_mate.start()
    own.wait()
    to_across.wait_recv()
    relay = send(slots.at[across], slots.at[across], gs.at[2], gr.at[2], (mate, tile))
    relay.start()
    to_mate.wait_recv()
    relay.wait_recv()

    def slot_of(cohort):
        where = 0
        for j in range(1, 4):
            where = where + j * (sched[j] == cohort).astype(jnp.int32)
        return jnp.minimum(where, 3)

    def pick(which, dst, offset):
        def one(x, carry):
            for f in range(5):
                dst[f, offset + x] = slots[which, f, pl.ds(x, 8, stride=8), :]
            return carry

        lax.fori_loop(0, TILE, one, 0)

    def spread(buf, s, r, halo):
        copies = []
        reach = min(halo, TILE)
        lo, hi = halo, halo + TILE
        copies.append((1, send(buf.at[:, pl.ds(hi - reach, reach)], buf.at[:, pl.ds(halo - reach, reach)], s.at[0], r.at[0], (sec, near[1]))))
        copies.append((-1, send(buf.at[:, pl.ds(lo, reach)], buf.at[:, pl.ds(hi, reach)], s.at[1], r.at[1], (sec, near[-1]))))
        rest = halo - reach
        if rest:
            copies.append((2, send(buf.at[:, pl.ds(hi - rest, rest)], buf.at[:, pl.ds(0, rest)], s.at[2], r.at[2], (sec, near[2]))))
            copies.append((-2, send(buf.at[:, pl.ds(lo, rest)], buf.at[:, pl.ds(hi + reach, rest)], s.at[3], r.at[3], (sec, near[-2]))))
        for _, c in copies:
            c.start()
        return [c for _, c in copies]

    def hand_over(buf, dst, s, r):
        copies = [
            send(buf.at[:, pl.ds(TILE - EDGE, EDGE)], dst.at[:, pl.ds(0, EDGE)], s.at[0], r.at[0], (mate, near[1])),
            send(buf.at[:, pl.ds(0, EDGE)], dst.at[:, pl.ds(EDGE + TILE, EDGE)], s.at[1], r.at[1], (mate, near[-1])),
            send(buf, dst.at[:, pl.ds(EDGE, TILE)], s.at[2], r.at[2], (mate, tile)),
        ]
        return copies

    pick(core * slot_of(1) + (1 - core) * slot_of(2), ext, HALO)
    halo1 = spread(ext, es, er, HALO)
    s0, s1, s2 = slopes.at[0], slopes.at[1], slopes.at[2]
    z0, z1, z2 = slopes0.at[0], slopes0.at[1], slopes0.at[2]
    to_core1 = hand_over(done2, lam, as_, ar)
    to_core0 = hand_over(done1, lam1, bs, br)
    final = send(out, out, fs, fr, (mate, tile))

    @pl.when(core == 0)
    def _():
        pick(slot_of(3), goal, EDGE)
        halo_t = spread(goal, ts, tr, EDGE)
        pick(slot_of(0), ext0, HALO)
        halo0 = spread(ext0, e0s, e0r, HALO)
        for c in halo1:
            c.wait_recv()
        first_stages(ext, first, second, s0, s1, 8)
        for c in halo_t:
            c.wait_recv()
        misfit(ext, second, s2, goal, lam)

        def emit2(f, x, value):
            done2[f, x] = value

        transposed_step(ext, first, second, s0, s1, s2, lam, g2, g1, emit2)
        for c in to_core1:
            c.start()
        for c in halo0:
            c.wait_recv()
        first_stages(ext0, first0, second0, z0, z1, 6)
        last_slopes(second0, z2)
        for c in to_core0:
            c.wait_recv()

        def emit0(f, x, value):
            out[f, pl.ds(x, 8, stride=8), :] = value

        transposed_step(ext0, first0, second0, z0, z1, z2, lam1, g2, g1, emit0)
        final.start()
        for c in halo_t + halo0 + to_core1:
            c.wait_send()
        final.wait_send()

    @pl.when(core == 1)
    def _():
        for c in halo1:
            c.wait_recv()
        first_stages(ext, first, second, s0, s1, 6)
        last_slopes(second, s2)
        for c in to_core1:
            c.wait_recv()

        def emit1(f, x, value):
            done1[f, x] = value

        transposed_step(ext, first, second, s0, s1, s2, lam, g2, g1, emit1)
        for c in to_core0:
            c.start()
        for c in to_core0:
            c.wait_send()
        final.wait_recv()

    for c in halo1:
        c.wait_send()
    to_across.wait_send()
    to_mate.wait_send()
    relay.wait_send()


def solution(mesh):
    tiles = mesh.shape["tile"]

    def body(saved, sched):
        local = saved.reshape(5, 64, 128)
        f32 = jnp.float32
        state = pltpu.VMEM((5, ROWS, 8, 128), f32)
        margin = pltpu.VMEM((5, LROWS, 8, 128), f32)
        block = pltpu.VMEM((5, TILE, 8, 128), f32)
        dma = pltpu.SemaphoreType.DMA
        result = pl.pallas_call(
            lambda *refs: kernel(tiles, *refs),
            out_shape=jax.ShapeDtypeStruct((5, 64, 128), f32),
            in_specs=[pl.BlockSpec(memory_space=pltpu.SMEM), pl.BlockSpec(memory_space=pl.ANY)],
            out_specs=pl.BlockSpec(memory_space=pltpu.VMEM),
            scratch_shapes=[
                pltpu.VMEM((4, 5, 64, 128), f32),
                state, state, margin,
                state, state, pltpu.VMEM((3, 12, ROWS, 8, 128), f32),
                state, state, pltpu.VMEM((3, 12, ROWS, 8, 128), f32),
                margin, margin, block, block, margin, margin,
                dma, dma((3,)), dma((3,)), dma((4,)), dma((4,)), dma((4,)), dma((4,)),
                dma((2,)), dma((2,)), dma((3,)), dma((3,)), dma((3,)), dma((3,)), dma, dma,
            ],
            compiler_params=pltpu.CompilerParams(collective_id=0, has_side_effects=True, vmem_limit_bytes=48 * 1024 * 1024),
            name="adjoint",
        )(sched, local)
        return result.reshape(5, 8, 8, 128)

    placed = (P("section", None, None, "tile", None), P())
    return jax.shard_map(body, mesh=mesh, in_specs=placed, out_specs=P(None, None, "tile", None), check_vma=False)
```

profile of v0, /device:TPU:1, one launch (start us, length us, event | category | flops | bytes accessed | tf_op | source)
XLA Modules:
  0.0 55.7 jit_solution(1887691779997431277)
XLA Ops:
  0.0 0.0 copy-start.1
  0.0 0.7 %copy-done.1 = s32[4]{0:T(128)S(1)} copy-done((s32[4]{0:T(128)S(1)}, s32[4]{0:T(128)}, u32[]{:S(2)}) %copy-start.1) | copy-done | bytes 40
  0.7 0.0 copy-start
  0.7 0.9 %copy-done = f32[1,5,8,8,128]{4,3,2,1,0:T(8,128)S(1)} copy-done((f32[1,5,8,8,128]{4,3,2,1,0:T(8,128)S(1)}, f32[1,5,8,8,128]{4,3,2,1,0:T(8,128)}, u32[]{:S(2)}) %copy-start) | copy-done | bytes 163864
  1.6 53.4 %adjoint.1 = f32[5,64,128]{2,1,0:T(8,128)S(1)} custom-call(s32[4]{0:T(128)S(1)} %copy-done.1, f32[5,64,128]{2,1,0:T(8,128)S(1)} %bitcast.3), custom_call_target="tpu_custom_call" | custom-call | tf_op jit(solution)/shard_map/adjoint/pallas_call | solution.py:341
  55.0 0.7 %copy.4 = f32[5,8,8,128]{3,2,1,0:T(8,128)} copy(f32[5,8,8,128]{3,2,1,0:T(8,128)S(1)} %bitcast.2) | data formatting | bytes 327680
Async XLA Ops:
  0.0 0.7 %copy-start.1 = (s32[4]{0:T(128)S(1)}, s32[4]{0:T(128)}, u32[]{:S(2)}) copy-start(s32[4]{0:T(128)} %refs_0_.1) | copy-start | bytes 52
  0.7 0.9 %copy-start = (f32[1,5,8,8,128]{4,3,2,1,0:T(8,128)S(1)}, f32[1,5,8,8,128]{4,3,2,1,0:T(8,128)}, u32[]{:S(2)}) copy-start(f32[1,5,8,8,128]{4,3,2,1,0:T(8,128)} %param.2) | copy-start | bytes 491524
where the time goes:
time: 55.8 us; the launch traced here: 55.7 us
  Pallas kernels  53.4 us (96%)
  local copies, waits for them, and re-layouts  2.24 us (4%)
    pallas_call x1, Pallas kernels, body(): pl.pallas_call(lambda *refs: kernel(tiles, *refs), out_shape=jax.ShapeDty...  53.4 us
    unnamed x5, local copies, waits for them, and re-layouts  2.24 us

commit v1 on v0

v1 whole, which is shorter than its diff:
```python
import jax
import jax.numpy as jnp
from jax import lax
from jax.experimental import pallas as pl
from jax.experimental.pallas import tpu as pltpu
from jax.sharding import PartitionSpec as P

MESH = pl.DeviceIdType.MESH

DT = 0.1
HYPER = 0.1
HALO = 6
TILE = 8
ROWS = TILE + 2 * HALO
U, V, W, B, PR = range(5)

D8 = 8.0 / 12.0
D1 = 1.0 / 12.0
C1 = DT * HYPER
C4 = 4.0 * C1
C0 = 18.0 * C1


def lanes(v, k):
    return pltpu.roll(v, (-k) % 128, 1)


def planes(v, k):
    return pltpu.roll(v, (-k) % 8, 0)


def slope_parts(p1, m1, p2, m2):
    return D8 * (p1 - m1) - D1 * (p2 - m2)


def forward_row(src, i, slopes, want_rate):
    mid = [src[f, i] for f in range(5)]
    vel = mid[:3]
    rate = [None] * 5
    dxs, dys, dzs = [], [], []
    for f in range(5):
        q = mid[f]
        xp1, xm1, xp2, xm2 = src[f, i + 1], src[f, i - 1], src[f, i + 2], src[f, i - 2]
        yp1, ym1, yp2, ym2 = lanes(q, 1), lanes(q, -1), lanes(q, 2), lanes(q, -2)
        zp1, zm1, zp2, zm2 = planes(q, 1), planes(q, -1), planes(q, 2), planes(q, -2)
        dx = slope_parts(xp1, xm1, xp2, xm2)
        dy = slope_parts(yp1, ym1, yp2, ym2)
        dz = slope_parts(zp1, zm1, zp2, zm2)
        dxs.append(dx)
        dys.append(dy)
        dzs.append(dz)
        if slopes is not None and f < 4:
            slopes[f, i] = dx
            slopes[4 + f, i] = dy
            slopes[8 + f, i] = dz
        if want_rate:
            near = ((xp1 + xm1) + (yp1 + ym1)) + (zp1 + zm1)
            far = ((xp2 + xm2) + (yp2 + ym2)) + (zp2 + zm2)
            rate[f] = C4 * near - C1 * far - C0 * q
    if not want_rate:
        return None, None
    vd = [DT * c for c in vel]
    for f in range(4):
        rate[f] = rate[f] - (vd[0] * dxs[f] + vd[1] * dys[f] + vd[2] * dzs[f])
    rate[U] = rate[U] - DT * dxs[PR]
    rate[V] = rate[V] - DT * dys[PR]
    rate[W] = rate[W] - DT * (dzs[PR] - mid[B])
    rate[B] = rate[B] - vd[2]
    rate[PR] = rate[PR] - DT * ((dxs[U] + dys[V]) + dzs[W])
    return mid, rate


def transposed_row(adj, base, slopes, i):
    at = i
    a = [adj[f, at] for f in range(5)]
    u_rows = {k: base[U, i + k] for k in (-2, -1, 1, 2)}
    u8p, u8m = (DT * D8) * u_rows[1], (DT * D8) * u_rows[-1]
    u1p, u1m = (DT * D1) * u_rows[2], (DT * D1) * u_rows[-2]
    v, w = base[V, i], base[W, i]
    v8, v1 = (DT * D8) * v, (DT * D1) * v
    w8, w1 = (DT * D8) * w, (DT * D1) * w
    ap = {k: adj[PR, at + k] for k in (-2, -1, 1, 2)}
    out = []
    for f in range(5):
        q = a[f]
        row = ap if f == PR else {k: adj[f, at + k] for k in (-2, -1, 1, 2)}
        total = C4 * (row[1] + row[-1]) - C1 * (row[2] + row[-2]) - C0 * q
        if f < 4:
            total = total + ((u8p * row[1] - u8m * row[-1]) - (u1p * row[2] - u1m * row[-2]))
            if f == U:
                total = total + ((DT * D8) * (ap[1] - ap[-1]) - (DT * D1) * (ap[2] - ap[-2]))
        else:
            au = {k: adj[U, at + k] for k in (-2, -1, 1, 2)}
            total = total + ((DT * D8) * (au[1] - au[-1]) - (DT * D1) * (au[2] - au[-2]))
        near, far = C4 * q, C1 * q
        if f < 4:
            p8, p1 = v8 * q, v1 * q
            if f == V:
                p8, p1 = p8 + (DT * D8) * a[PR], p1 + (DT * D1) * a[PR]
        else:
            p8, p1 = (DT * D8) * a[V], (DT * D1) * a[V]
        total = total + (lanes(near + p8, 1) + lanes(near - p8, -1))
        total = total - (lanes(far + p1, 2) + lanes(far - p1, -2))
        if f < 4:
            p8, p1 = w8 * q, w1 * q
            if f == W:
                p8, p1 = p8 + (DT * D8) * a[PR], p1 + (DT * D1) * a[PR]
        else:
            p8, p1 = (DT * D8) * a[W], (DT * D1) * a[W]
        total = total + (planes(near + p8, 1) + planes(near - p8, -1))
        total = total - (planes(far + p1, 2) + planes(far - p1, -2))
        out.append(total)
    ad = [DT * c for c in a[:4]]
    for d in range(3):
        s = ad[0] * slopes[4 * d, i] + ad[1] * slopes[4 * d + 1, i]
        s = s + (ad[2] * slopes[4 * d + 2, i] + ad[3] * slopes[4 * d + 3, i])
        out[d] = out[d] - s
    out[W] = out[W] - ad[3]
    out[B] = out[B] + ad[2]
    return a, out


def margin_row(adj, base, i, offsets):
    out = [None] * 5
    for k in offsets:
        near = abs(k) == 1
        size = D8 if near else -D1
        slope = DT * size if k > 0 else -DT * size
        hyper = C4 if near else -C1
        a = [adj[f, i + k] for f in range(5)]
        speed = slope * base[U, i + k] + hyper
        for f in range(5):
            term = speed * a[f] if f < 4 else hyper * a[f]
            if f == U:
                term = term + slope * a[PR]
            if f == PR:
                term = term + slope * a[U]
            out[f] = term if out[f] is None else out[f] + term
    return out


def margins(adj, base, lo, hi, put):
    for i, offsets in ((lo - 2, (2,)), (lo - 1, (1, 2)), (hi, (-1, -2)), (hi + 1, (-2,))):
        put(i, margin_row(adj, base, i, offsets))


def rows_loop(lo, hi, body):
    def step(j, carry):
        i = lo + 2 * j
        body(i)
        body(i + 1)
        return carry

    lax.fori_loop(0, (hi - lo) // 2, step, 0)


LO, HI = HALO, HALO + TILE


def first_stages(state, first, second, s0, s1):
    def one(i):
        mid, rate = forward_row(state, i, s0, True)
        for f in range(5):
            first[f, i] = mid[f] + rate[f]

    rows_loop(LO - 4, HI + 4, one)

    def two(i):
        mid, rate = forward_row(first, i, s1, True)
        for f in range(5):
            second[f, i] = 0.75 * state[f, i] + 0.25 * (mid[f] + rate[f])

    rows_loop(LO - 2, HI + 2, two)


def last_slopes(second, s2):
    def three(i):
        forward_row(second, i, s2, False)

    rows_loop(LO, HI, three)


def misfit(state, second, s2, slots, goal, lam):
    def three(i):
        mid, rate = forward_row(second, i, s2, True)
        for f in range(5):
            end = state[f, i] / 3.0 + (2.0 / 3.0) * (mid[f] + rate[f])
            lam[f, i] = end - slots[goal, f, pl.ds(i - LO, 8, stride=8), :]

    rows_loop(LO, HI, three)


def clear(buf, width):
    for f in range(5):
        for i in range(width):
            buf[f, i] = jnp.zeros((8, 128), jnp.float32)
            buf[f, ROWS - 1 - i] = jnp.zeros((8, 128), jnp.float32)


def transposed_step(state, first, second, s0, s1, s2, lam, g2, g1, gq, edges_done):
    def three(i):
        a, out = transposed_row(lam, second, s2, i)
        for f in range(5):
            g2[f, i] = (2.0 / 3.0) * (a[f] + out[f])

    def put2(i, out):
        for f in range(5):
            g2[f, i] = (2.0 / 3.0) * out[f]

    margins(lam, second, LO, HI, put2)
    rows_loop(LO, HI, three)

    def two(i):
        a, out = transposed_row(g2, first, s1, i)
        for f in range(5):
            g1[f, i] = 0.25 * (a[f] + out[f])

    def put1(i, out):
        for f in range(5):
            g1[f, i] = 0.25 * out[f]

    margins(g2, first, LO - 2, HI + 2, put1)
    rows_loop(LO - 2, HI + 2, two)

    def one(i):
        a, out = transposed_row(g1, state, s0, i)
        for f in range(5):
            gq[f, i] = lam[f, i] / 3.0 + 0.75 * g2[f, i] + (a[f] + out[f])

    def put0(i, out):
        for f in range(5):
            gq[f, i] = out[f]

    margins(g1, state, LO - 4, HI + 4, put0)

    def edge(j, carry):
        one(LO - 4 + j)
        one(HI + j)
        return carry

    lax.fori_loop(0, 4, edge, 0)
    edges_done()
    rows_loop(LO, HI, one)


def collect(parts, put):
    middle, before, after = parts
    for x in range(TILE):
        for f in range(5):
            total = middle(f, x)
            if x < HALO:
                total = total + before[f, x]
            if x >= TILE - HALO:
                total = total + after[f, x - (TILE - HALO)]
            put(f, x, total)


def kernel(tiles, sched_in, saved, out, sched, sched_sem, slots, ext, ext0, first, second, slopes, first0, second0, slopes0, lam, g2, g1, gq, gq0,
           mid_in, mid_last, before_in, after_in, before_last, after_last,
           own_sem, gs, gr, es, er, e0s, e0r, as_, ar, fs, fr, go):
    sec, tile = lax.axis_index("section"), lax.axis_index("tile")
    core = lax.rem(sec, 2)
    mate = sec + 1 - 2 * core
    half = lax.div(sec, 2)
    across = sec + 2 - 4 * half
    right, left = lax.rem(tile + 1, tiles), lax.rem(tile + tiles - 1, tiles)

    own = pltpu.make_async_copy(saved, slots.at[sec], own_sem)
    own.start()
    order = pltpu.make_async_copy(sched_in, sched, sched_sem)
    order.start()

    barrier = pltpu.get_barrier_semaphore()
    partners = [(mate, tile), (across, tile), (sec, left), (sec, right), (mate, left), (mate, right)]
    for who in partners:
        pl.semaphore_signal(barrier, inc=1, device_id=who, device_id_type=MESH)
    clear(lam, 6)
    clear(g2, 4)
    clear(g1, 2)
    pl.semaphore_wait(barrier, len(partners))

    def send(src, dst, s, r, who):
        return pltpu.make_async_remote_copy(src_ref=src, dst_ref=dst, send_sem=s, recv_sem=r, device_id=who, device_id_type=MESH)

    to_across = send(saved, slots.at[sec], gs.at[0], gr.at[0], (across, tile))
    to_mate = send(saved, slots.at[sec], gs.at[1], gr.at[1], (mate, tile))
    to_across.start()
    to_mate.start()
    own.wait()
    order.wait()
    to_across.wait_recv()
    relay = send(slots.at[across], slots.at[across], gs.at[2], gr.at[2], (mate, tile))
    relay.start()
    to_mate.wait_recv()
    relay.wait_recv()

    def slot_of(cohort):
        where = 0
        for j in range(1, 4):
            where = where + j * (sched[j] == cohort).astype(jnp.int32)
        return jnp.minimum(where, 3)

    def pick(which, dst):
        def one(x, carry):
            for f in range(5):
                dst[f, LO + x] = slots[which, f, pl.ds(x, 8, stride=8), :]
            return carry

        lax.fori_loop(0, TILE, one, 0)

    def spread(buf, s, r):
        copies = [
            send(buf.at[:, pl.ds(HI - HALO, HALO)], buf.at[:, pl.ds(0, HALO)], s.at[0], r.at[0], (sec, right)),
            send(buf.at[:, pl.ds(LO, HALO)], buf.at[:, pl.ds(HI, HALO)], s.at[1], r.at[1], (sec, left)),
        ]
        return copies

    def push_edges(buf, before, after, s, r, to, k):
        return [
            send(buf.at[:, pl.ds(HI, HALO)], before, s.at[k], r.at[k], (to, right)),
            send(buf.at[:, pl.ds(0, HALO)], after, s.at[k + 1], r.at[k + 1], (to, left)),
        ]

    def start(copies):
        for c in copies:
            c.start()

    def received(copies):
        for c in copies:
            c.wait_recv()

    def sent(copies):
        for c in copies:
            c.wait_send()

    s0, s1, s2 = slopes.at[0], slopes.at[1], slopes.at[2]
    z0, z1, z2 = slopes0.at[0], slopes0.at[1], slopes0.at[2]
    halo1, halo0 = spread(ext, es, er), spread(ext0, e0s, e0r)
    edges = push_edges(gq, before_in, after_in, as_, ar, mate, 0)
    centre = send(gq.at[:, pl.ds(LO, TILE)], mid_in, as_.at[2], ar.at[2], (mate, tile))
    last_own = push_edges(gq0, before_last, after_last, fs, fr, sec, 0)
    last_mate = push_edges(gq0, before_last, after_last, fs, fr, mate, 2)
    last_centre = send(gq0.at[:, pl.ds(LO, TILE)], mid_last, fs.at[4], fr.at[4], (mate, tile))

    def put_lam(f, x, value):
        lam[f, LO + x] = value

    def put_out(f, x, value):
        out[f, pl.ds(x, 8, stride=8), :] = value

    pick(core * slot_of(1) + (1 - core) * slot_of(2), ext)

    @pl.when(core == 0)
    def _():
        start(halo1)
        pick(slot_of(0), ext0)
        received(halo1)
        sent(halo1)
        pl.semaphore_signal(go, inc=1, device_id=(mate, tile), device_id_type=MESH)
        start(halo0)
        first_stages(ext, first, second, s0, s1)
        misfit(ext, second, s2, slots, slot_of(3), lam)
        transposed_step(ext, first, second, s0, s1, s2, lam, g2, g1, gq, lambda: start(edges))
        centre.start()
        received(halo0)
        first_stages(ext0, first0, second0, z0, z1)
        last_slopes(second0, z2)
        received(edges + [centre])
        collect((lambda f, x: mid_in[f, x], before_in, after_in), put_lam)
        transposed_step(ext0, first0, second0, z0, z1, z2, lam, g2, g1, gq0, lambda: start(last_own + last_mate))
        last_centre.start()
        received(last_own)
        collect((lambda f, x: gq0[f, LO + x], before_last, after_last), put_out)
        sent(halo0 + edges + [centre] + last_own + last_mate + [last_centre])

    @pl.when(core == 1)
    def _():
        pl.semaphore_wait(go, 1)
        start(halo1)
        received(halo1)
        first_stages(ext, first, second, s0, s1)
        last_slopes(second, s2)
        received(edges + [centre])
        collect((lambda f, x: mid_in[f, x], before_in, after_in), put_lam)
        transposed_step(ext, first, second, s0, s1, s2, lam, g2, g1, gq, lambda: start(edges))
        centre.start()
        received(last_mate + [last_centre])
        collect((lambda f, x: mid_last[f, x], before_last, after_last), put_out)
        sent(halo1 + edges + [centre])

    sent([to_across, to_mate, relay])


def solution(mesh):
    tiles = mesh.shape["tile"]

    def body(saved, sched):
        local = saved.reshape(5, 64, 128)
        f32 = jnp.float32
        state = pltpu.VMEM((5, ROWS, 8, 128), f32)
        block = pltpu.VMEM((5, TILE, 8, 128), f32)
        margin = pltpu.VMEM((5, HALO, 8, 128), f32)
        slopes = pltpu.VMEM((3, 12, ROWS, 8, 128), f32)
        dma = pltpu.SemaphoreType.DMA
        result = pl.pallas_call(
            lambda *refs: kernel(tiles, *refs),
            out_shape=jax.ShapeDtypeStruct((5, 64, 128), f32),
            in_specs=[pl.BlockSpec(memory_space=pltpu.HBM), pl.BlockSpec(memory_space=pltpu.HBM)],
            out_specs=pl.BlockSpec(memory_space=pltpu.VMEM),
            scratch_shapes=[
                pltpu.SMEM((4,), jnp.int32), pltpu.SemaphoreType.DMA,
                pltpu.VMEM((4, 5, 64, 128), f32),
                state, state, state, state, slopes, state, state, slopes,
                state, state, state, state, state,
                block, block, margin, margin, margin, margin,
                dma, dma((3,)), dma((3,)), dma((2,)), dma((2,)), dma((2,)), dma((2,)),
                dma((3,)), dma((3,)), dma((5,)), dma((5,)), pltpu.SemaphoreType.REGULAR,
            ],
            compiler_params=pltpu.CompilerParams(collective_id=0, has_side_effects=True, vmem_limit_bytes=48 * 1024 * 1024),
            name="adjoint",
        )(sched, local)
        return result.reshape(5, 8, 8, 128)

    placed = (P("section", None, None, "tile", None), P())
    return jax.shard_map(body, mesh=mesh, in_specs=placed, out_specs=P(None, None, "tile", None), check_vma=False)
```

time: 55.8 us -> 53.7 us (0.962)
  Pallas kernels: 53.4 us -> 51.4 us
    pallas_call x1, Pallas kernels: 53.4 us -> 51.4 us  [body(): pl.pallas_call(lambda *refs: kernel(tiles, *refs), out_shape=jax.ShapeDty...]
where the time goes in v1:
time: 53.7 us; the launch traced here: 53.6 us
  Pallas kernels  51.4 us (96%)
  local copies, waits for them, and re-layouts  2.24 us (4%)
    pallas_call x1, Pallas kernels, body(): pl.pallas_call(lambda *refs: kernel(tiles, *refs), out_shape=jax.ShapeDty...  51.4 us
    unnamed x5, local copies, waits for them, and re-layouts  2.24 us

profile of v1, /device:TPU:1, one launch (start us, length us, event | category | flops | bytes accessed | tf_op | source)
XLA Modules:
  0.0 53.6 jit_solution(8840798904508128230)
XLA Ops:
  0.0 0.0 copy-start.1
  0.0 0.7 %copy-done.1 = s32[4]{0:T(128)S(1)} copy-done((s32[4]{0:T(128)S(1)}, s32[4]{0:T(128)}, u32[]{:S(2)}) %copy-start.1) | copy-done | bytes 40
  0.7 0.0 copy-start
  0.7 0.9 %copy-done = f32[1,5,8,8,128]{4,3,2,1,0:T(8,128)S(1)} copy-done((f32[1,5,8,8,128]{4,3,2,1,0:T(8,128)S(1)}, f32[1,5,8,8,128]{4,3,2,1,0:T(8,128)}, u32[]{:S(2)}) %copy-start) | copy-done | bytes 163864
  1.6 51.4 %adjoint.1 = f32[5,64,128]{2,1,0:T(8,128)S(1)} custom-call(s32[4]{0:T(128)S(1)} %copy-done.1, f32[5,64,128]{2,1,0:T(8,128)S(1)} %bitcast.3), custom_call_target="tpu_custom_call" | custom-call | tf_op jit(solution)/shard_map/adjoint/pallas_call | solution.py:405
  52.9 0.7 %copy.4 = f32[5,8,8,128]{3,2,1,0:T(8,128)} copy(f32[5,8,8,128]{3,2,1,0:T(8,128)S(1)} %bitcast.2) | data formatting | bytes 327680
Async XLA Ops:
  0.0 0.7 %copy-start.1 = (s32[4]{0:T(128)S(1)}, s32[4]{0:T(128)}, u32[]{:S(2)}) copy-start(s32[4]{0:T(128)} %refs_0_.1) | copy-start | bytes 52
  0.7 0.9 %copy-start = (f32[1,5,8,8,128]{4,3,2,1,0:T(8,128)S(1)}, f32[1,5,8,8,128]{4,3,2,1,0:T(8,128)}, u32[]{:S(2)}) copy-start(f32[1,5,8,8,128]{4,3,2,1,0:T(8,128)} %param.2) | copy-start | bytes 491524
